TPU v7x, 32 devices: a whole 2x2x4 slice. The times are simulated.
32 devices in a mesh: row: 8 (over z, y), feat: 4 (over x, core).
Axes of the slice: x: 2, y: 2, z: 4, core: 2. Of those that a mesh axis runs over, the one named last changes fastest.
Arguments:
- design: bfloat16 [1024, 65536], P('row', 'feat'), may hold values from -0.0234375 to 0.0234375
- targets: bfloat16 [1024, 48], P('row'), may hold values from -6 to 6
- factor: float32 [65536, 256], P(('feat', 'row')), may hold values from -0.09375 to 0.09375
- weights: float32 [256], replicated, may hold values from 0.3 to 3
- penalty: float32 [48], replicated, may hold values from 0.05 to 0.5
Outputs:
- solution: float32 [65536, 48], P(('feat', 'row'))
- residual: float32 [65536, 48], P(('feat', 'row'))
All inputs are finite; a program needn't handle non-finite values.
Results may differ from a plain program's by a relative error of at most 0.024.
Values may be sent and summed in bfloat16 or wider, within the bound.
A program may use at most 64 MiB of HBM per device.

v0:
```python
import jax
import jax.numpy as jnp
from jax import lax
from jax.sharding import PartitionSpec as P

ITERS = 3


def shards(design, targets, factor, weights, penalty):

    def normal_terms(rows_low):
        return lax.psum_scatter(
            lax.dot_general(
                design, rows_low, (((0,), (0,)), ((), ())), preferred_element_type=jnp.float32
            ),
            "row",
            scatter_dimension=0,
            tiled=True,
        )

    def precondition(residual):
        projected = jnp.dot(factor.T, residual, precision=lax.Precision.HIGHEST)
        projected = lax.psum(projected, ("row", "feat"))
        search = residual + jnp.dot(
            factor, weights[:, None] * projected, precision=lax.Precision.HIGHEST
        )
        inner = lax.psum(jnp.sum(residual * search, axis=0), ("row", "feat"))
        return (search, inner)

    residual = normal_terms(targets)
    solution = jnp.zeros_like(residual)
    search, inner = precondition(residual)
    direction = search
    for step_index in range(ITERS):
        dir_low = direction.astype(jnp.bfloat16)
        row_values = lax.psum(
            jnp.dot(
                design,
                lax.all_gather(dir_low, "row", axis=0, tiled=True),
                preferred_element_type=jnp.float32,
            ),
            "feat",
        )
        row_low = row_values.astype(jnp.bfloat16)
        dir_slice = direction
        local_part = jnp.sum(row_values * row_low.astype(jnp.float32), axis=0) / lax.axis_size(
            "feat"
        )
        local_part = local_part + penalty * jnp.sum(dir_slice * dir_slice, axis=0)
        curvature = lax.psum(local_part, ("row", "feat"))
        hessian_dir = normal_terms(row_low) + penalty[None, :] * dir_slice
        step_size = inner / curvature
        solution = solution + step_size[None, :] * dir_slice
        residual = residual - step_size[None, :] * hessian_dir
        if step_index + 1 < ITERS:
            search, inner_next = precondition(residual)
            direction = search + (inner_next / inner)[None, :] * direction
            inner = inner_next
    return (solution, residual)


def solution(mesh):
    return jax.shard_map(
        shards,
        mesh=mesh,
        in_specs=(P("row", "feat"), P("row", None), P(("feat", "row"), None), P(), P()),
        out_specs=(P(("feat", "row"), None), P(("feat", "row"), None)),
        check_vma=False,
    )
```

profile of v0, /device:TPU:0, one launch (start us, length us, event | category | flops | bytes accessed | tf_op | source)
XLA Modules:
  0.0 737.3 jit_solution(17198309492776830987)
XLA Ops:
  7.2 4.7 fusion.13
  12.0 77.5 %reduce-scatter.5.cloned.1.call-done = f32[2048,48]{0,1:T(8,128)} async-done(((f32[16384,48]{0,1:T(8,128)}), f32[2048,48]{0,1:T(8,128)}) %reduce-scatter.5.cloned.1.call-update) | async-done | bytes 393232 | tf_op jit(solution)/shard_map/reduce_scatter | solution.py:12
  89.6 4.5 convolution_bitcast_fusion.8
  94.1 40.7 %psum.84 = f32[256,48]{1,0:T(8,128)S(1)} all-reduce(f32[256,48]{1,0:T(8,128)S(1)} %convolution_bitcast_fusion.8), channel_id=1, replica_groups=mesh['row'=8,'feat'=4] {'row','feat'}, use_global_device_ids=true, to_apply=%region_1.0 | all-reduce | flops 12288 | bytes 98304 | tf_op jit(solution)/shard_map/psum | solution.py:23
  137.6 43.6 %all-gather.4.cloned.1.call-done = bf16[16384,48]{0,1:T(8,128)(2,1)} async-done(((bf16[2048,48]{0,1:T(8,128)(2,1)}), bf16[16384,48]{0,1:T(8,128)(2,1)}) %all-gather.4.cloned.1.call-update) | async-done | bytes 1572880 | tf_op jit(solution)/shard_map/all_gather | solution.py:39
  185.4 10.3 %psum.86 = f32[128,48]{0,1:T(8,128)S(1)} all-reduce(f32[128,48]{0,1:T(8,128)S(1)} %convolution_bitcast_fusion.11), channel_id=1, replica_groups=mesh['row'=8,'feat'=4] {'feat'}, use_global_device_ids=true, to_apply=%region_4.0 | all-reduce | flops 6144 | bytes 49152 | tf_op jit(solution)/shard_map/psum | solution.py:36
  195.7 4.5 convolution_bitcast_fusion.2
  200.9 40.9 %all-reduce = (f32[48]{0:T(128)S(1)}, f32[48]{0:T(128)S(1)}) all-reduce(f32[48]{0:T(128)S(1)} %get-tuple-element.3, f32[48]{0:T(128)S(1)} %multiply_add_fusion.5), channel_id=1, replica_groups=mesh['row'=8,'feat'=4] {'row','feat'}, use_global_device_ids=true, to_apply=%region_3.0 | all-reduce | flops 96 | bytes 768 | tf_op jit(solution)/shard_map/psum | solution.py:27
  241.8 33.1 %reduce-scatter.7.cloned.1.call-done = f32[2048,48]{0,1:T(8,128)} async-done(((f32[16384,48]{0,1:T(8,128)}), f32[2048,48]{0,1:T(8,128)}) %reduce-scatter.7.cloned.1.call-update) | async-done | bytes 393232 | tf_op jit(solution)/shard_map/reduce_scatter | solution.py:12
  279.5 40.7 %psum.88 = f32[256,48]{1,0:T(8,128)S(1)} all-reduce(f32[256,48]{1,0:T(8,128)S(1)} %convolution_bitcast_fusion.7), channel_id=1, replica_groups=mesh['row'=8,'feat'=4] {'row','feat'}, use_global_device_ids=true, to_apply=%region_9.0 | all-reduce | flops 12288 | bytes 98304 | tf_op jit(solution)/shard_map/psum | solution.py:23
  323.0 39.4 %psum.89 = f32[48]{0:T(128)S(1)} all-reduce(f32[48]{0:T(128)S(1)} %get-tuple-element.14), channel_id=1, replica_groups=mesh['row'=8,'feat'=4] {'row','feat'}, use_global_device_ids=true, to_apply=%region_11.0 | all-reduce | flops 48 | bytes 384 | tf_op jit(solution)/shard_map/psum | solution.py:27
  364.5 44.2 %all-gather.6.cloned.1.call-done = bf16[16384,48]{0,1:T(8,128)(2,1)} async-done(((bf16[2048,48]{0,1:T(8,128)(2,1)}), bf16[16384,48]{0,1:T(8,128)(2,1)}) %all-gather.6.cloned.1.call-update) | async-done | bytes 1572880 | tf_op jit(solution)/shard_map/all_gather | solution.py:39
  408.7 4.2 convolution_bitcast_fusion.10
  412.9 10.3 %psum.90 = f32[128,48]{0,1:T(8,128)S(1)} all-reduce(f32[128,48]{0,1:T(8,128)S(1)} %convolution_bitcast_fusion.10), channel_id=1, replica_groups=mesh['row'=8,'feat'=4] {'feat'}, use_global_device_ids=true, to_apply=%region_12.0 | all-reduce | flops 6144 | bytes 49152 | tf_op jit(solution)/shard_map/psum | solution.py:36
  423.2 4.5 convolution_bitcast_fusion.1
  427.9 41.2 %psum.91 = f32[48]{0:T(128)S(1)} all-reduce(f32[48]{0:T(128)S(1)} %multiply_add_fusion.4), channel_id=1, replica_groups=mesh['row'=8,'feat'=4] {'row','feat'}, use_global_device_ids=true, to_apply=%region_15.0 | all-reduce | flops 48 | bytes 384 | tf_op jit(solution)/shard_map/psum | solution.py:50
  469.1 33.4 %reduce-scatter.9.cloned.1.call-done = f32[2048,48]{0,1:T(8,128)} async-done(((f32[16384,48]{0,1:T(8,128)}), f32[2048,48]{0,1:T(8,128)}) %reduce-scatter.9.cloned.1.call-update) | async-done | bytes 393232 | tf_op jit(solution)/shard_map/reduce_scatter | solution.py:12
  507.0 40.7 %psum.92 = f32[256,48]{1,0:T(8,128)S(1)} all-reduce(f32[256,48]{1,0:T(8,128)S(1)} %convolution_bitcast_fusion.6), channel_id=1, replica_groups=mesh['row'=8,'feat'=4] {'row','feat'}, use_global_device_ids=true, to_apply=%region_17.0 | all-reduce | flops 12288 | bytes 98304 | tf_op jit(solution)/shard_map/psum | solution.py:23
  549.8 39.4 %psum.93 = f32[48]{0:T(128)S(1)} all-reduce(f32[48]{0:T(128)S(1)} %get-tuple-element.16), channel_id=1, replica_groups=mesh['row'=8,'feat'=4] {'row','feat'}, use_global_device_ids=true, to_apply=%region_19.0 | all-reduce | flops 48 | bytes 384 | tf_op jit(solution)/shard_map/psum | solution.py:27
  590.2 44.2 %all-gather.8.cloned.1.call-done = bf16[16384,48]{0,1:T(8,128)(2,1)} async-done(((bf16[2048,48]{0,1:T(8,128)(2,1)}), bf16[16384,48]{0,1:T(8,128)(2,1)}) %all-gather.8.cloned.1.call-update) | async-done | bytes 1572880 | tf_op jit(solution)/shard_map/all_gather | solution.py:39
  638.6 10.3 %psum.94 = f32[128,48]{0,1:T(8,128)S(1)} all-reduce(f32[128,48]{0,1:T(8,128)S(1)} %convolution_bitcast_fusion.9), channel_id=1, replica_groups=mesh['row'=8,'feat'=4] {'feat'}, use_global_device_ids=true, to_apply=%region_20.0 | all-reduce | flops 6144 | bytes 49152 | tf_op jit(solution)/shard_map/psum | solution.py:36
  648.9 4.5 convolution_bitcast_fusion
  654.8 41.2 %psum.95 = f32[48]{0:T(128)S(1)} all-reduce(f32[48]{0:T(128)S(1)} %multiply_add_fusion.3), channel_id=1, replica_groups=mesh['row'=8,'feat'=4] {'row','feat'}, use_global_device_ids=true, to_apply=%region_23.0 | all-reduce | flops 48 | bytes 384 | tf_op jit(solution)/shard_map/psum | solution.py:50
  696.0 32.2 %reduce-scatter.11.cloned.1.call-done = f32[2048,48]{0,1:T(8,128)} async-done(((f32[16384,48]{0,1:T(8,128)}), f32[2048,48]{0,1:T(8,128)}) %reduce-scatter.11.cloned.1.call-update) | async-done | bytes 393232 | tf_op jit(solution)/shard_map/reduce_scatter | solution.py:12
  (51 shorter events, 32.5 us)
Async XLA Ops:
  7.2 82.4 %copy-start = (f32[2048,256]{1,0:T(8,128)S(1)}, f32[2048,256]{1,0:T(8,128)}, u32[]{:S(2)}) copy-start(f32[2048,256]{1,0:T(8,128)} %param.7) | copy-start | bytes 6291460
  7.2 82.4 %reduce-scatter.5.cloned.1.call-start = ((), (), s32[]{:S(2)}) async-start(), calls=%async_computation.4 | async-start | bytes 3538944 | tf_op jit(solution)/shard_map/reduce_scatter | solution.py:12
  12.0 122.8 %copy-start.5 = (f32[256]{0:T(256)S(1)}, f32[256]{0:T(256)}, u32[]{:S(2)}) copy-start(f32[256]{0:T(256)} %param.8) | copy-start | bytes 3076
  12.0 169.2 %all-gather.4.cloned.1.call-start = ((), (), s32[]{:S(2)}) async-start(), calls=%async_computation.5 | async-start | bytes 1769472 | tf_op jit(solution)/shard_map/all_gather | solution.py:39
  89.6 45.2 %copy-start.3 = (f32[2048,48]{0,1:T(8,128)S(1)}, f32[2048,48]{0,1:T(8,128)}, u32[]{:S(2)}) copy-start(f32[2048,48]{0,1:T(8,128)} %reduce-scatter.5.cloned.1.call-done) | copy-start | bytes 1179652
  137.5 224.9 %copy-start.1 = (f32[2048,48]{0,1:T(8,128)}, f32[2048,48]{0,1:T(8,128)S(1)}, u32[]{:S(2)}) copy-start(f32[2048,48]{0,1:T(8,128)S(1)} %get-tuple-element.13) | copy-start | bytes 1179652
  137.6 137.4 %reduce-scatter.7.cloned.1.call-start = ((), (), s32[]{:S(2)}) async-start(), calls=%async_computation.6 | async-start | bytes 3538944 | tf_op jit(solution)/shard_map/reduce_scatter | solution.py:12
  200.2 0.7 copy-start.4
  200.3 208.4 %all-gather.6.cloned.1.call-start = ((), (), s32[]{:S(2)}) async-start(), calls=%async_computation.7 | async-start | bytes 1769472 | tf_op jit(solution)/shard_map/all_gather | solution.py:39
  364.4 138.0 %reduce-scatter.9.cloned.1.call-start = ((), (), s32[]{:S(2)}) async-start(), calls=%async_computation.8 | async-start | bytes 3538944 | tf_op jit(solution)/shard_map/reduce_scatter | solution.py:12
  427.7 206.7 %all-gather.8.cloned.1.call-start = ((), (), s32[]{:S(2)}) async-start(), calls=%async_computation.9 | async-start | bytes 1769472 | tf_op jit(solution)/shard_map/all_gather | solution.py:39
  590.1 138.1 %reduce-scatter.11.cloned.1.call-start = ((), (), s32[]{:S(2)}) async-start(), calls=%async_computation.10 | async-start | bytes 3538944 | tf_op jit(solution)/shard_map/reduce_scatter | solution.py:12
  653.4 74.8 %copy-start.2 = (f32[2048,48]{0,1:T(8,128)S(1)}, f32[2048,48]{0,1:T(8,128)}, u32[]{:S(2)}) copy-start(f32[2048,48]{0,1:T(8,128)} %copy-done.1) | copy-start | bytes 1179652
Sparse Core Ops, SparseCore 0:
  12.1 77.4 reduce-scatter.4
  137.7 43.4 all-gather.3
  200.4 74.5 reduce-scatter.6
  364.5 44.0 all-gather.5
  427.8 74.5 reduce-scatter.8
  590.2 44.1 all-gather.7
  653.6 74.6 reduce-scatter.10
where the time goes:
time: 739 us; the launch traced here: 737 us
  blocking collectives  355 us (48%)
  waiting for transfers between devices  308 us (42%)
  matrix products  49.8 us (7%)
  between operations  14.3 us (2%)
  other arithmetic  8.84 us (1%)
    reduce_scatter x4, waiting for transfers between devices, normal_terms(): lax.psum_scatter(lax.dot_general(design, rows_low, (((0,), (0,)), ((), ()...  176 us
    all_gather x3, waiting for transfers between devices, shards(): lax.all_gather(dir_low, 'row', axis=0, tiled=True)  132 us
    psum x3, blocking collectives, precondition(): projected = lax.psum(projected, ('row', 'feat'))  122 us
    psum x3, blocking collectives, precondition(): inner = lax.psum(jnp.sum(residual * search, axis=0), ('row', 'feat'))  120 us
    psum x2, blocking collectives, shards(): curvature = lax.psum(local_part, ('row', 'feat'))  82.4 us
    psum x3, blocking collectives, shards(): lax.psum(jnp.dot(design, lax.all_gather(dir_low, 'row', axis=0, tiled=Tru...  30.8 us
    dot_general x4, matrix products, normal_terms(): lax.dot_general(design, rows_low, (((0,), (0,)), ((), ())), preferred_ele...  18.3 us
  transfers between devices with their start and end apart: 7, of which 7 were waited for; matrix products, arithmetic and copies ran while one was open for 0% of the time, Pallas kernels for 0%

commit v1 on v0

--- a/solution.py
+++ b/solution.py
@@ -24,7 +24,7 @@
         search = residual + jnp.dot(
             factor, weights[:, None] * projected, precision=lax.Precision.HIGHEST
         )
-        inner = lax.psum(jnp.sum(residual * search, axis=0), ("row", "feat"))
+        inner = lax.psum(lax.psum(jnp.sum(residual * search, axis=0), "feat"), "row")
         return (search, inner)
 
     residual = normal_terms(targets)

time: 739 us -> 705 us (0.954)
  waiting for transfers between devices: 308 us -> 280 us
    psum x3 -> x5, blocking collectives: 120 us -> 73.5 us  [the longest x3 61.9 us: precondition(): lax.psum(lax.psum(jnp.sum(residual * search, axis=0), 'feat'), 'row')]
    psum x2 -> x3, blocking collectives: 82.4 us -> 124 us  [shards(): curvature = lax.psum(local_part, ('row', 'feat'))]
    reduce_scatter x4, waiting for transfers between devices: 176 us -> 155 us  [normal_terms(): lax.psum_scatter(lax.dot_general(design, rows_low, (((0,), (0,)), ((), ()...]
where the time goes in v1:
time: 705 us; the launch traced here: 704 us
  blocking collectives  350 us (50%)
  waiting for transfers between devices  280 us (40%)
  matrix products  49.8 us (7%)
  between operations  14.3 us (2%)
  other arithmetic  8.85 us (1%)
    reduce_scatter x4, waiting for transfers between devices, normal_terms(): lax.psum_scatter(lax.dot_general(design, rows_low, (((0,), (0,)), ((), ()...  155 us
    all_gather x3, waiting for transfers between devices, shards(): lax.all_gather(dir_low, 'row', axis=0, tiled=True)  125 us
    psum x3, blocking collectives, shards(): curvature = lax.psum(local_part, ('row', 'feat'))  124 us
    psum x3, blocking collectives, precondition(): projected = lax.psum(projected, ('row', 'feat'))  122 us
    psum x3, blocking collectives, precondition(): lax.psum(lax.psum(jnp.sum(residual * search, axis=0), 'feat'), 'row')  61.9 us
    psum x3, blocking collectives, shards(): lax.psum(jnp.dot(design, lax.all_gather(dir_low, 'row', axis=0, tiled=Tru...  30.8 us
    dot_general x4, matrix products, normal_terms(): lax.dot_general(design, rows_low, (((0,), (0,)), ((), ())), preferred_ele...  18.4 us
  transfers between devices with their start and end apart: 7, of which 7 were waited for; matrix products, arithmetic and copies ran while one was open for 0% of the time, Pallas kernels for 0%

profile of v1, /device:TPU:0, one launch (start us, length us, event | category | flops | bytes accessed | tf_op | source)
XLA Modules:
  0.0 703.9 jit_solution(8218213012270531250)
XLA Ops:
  7.2 4.7 fusion.13
  12.0 77.5 %reduce-scatter.5.cloned.1.call-done = f32[2048,48]{0,1:T(8,128)} async-done(((f32[16384,48]{0,1:T(8,128)}), f32[2048,48]{0,1:T(8,128)}) %reduce-scatter.5.cloned.1.call-update) | async-done | bytes 393232 | tf_op jit(solution)/shard_map/reduce_scatter | solution.py:12
  94.1 40.7 %psum.105 = f32[256,48]{1,0:T(8,128)S(1)} all-reduce(f32[256,48]{1,0:T(8,128)S(1)} %convolution_bitcast_fusion.8), channel_id=1, replica_groups=mesh['row'=8,'feat'=4] {'row','feat'}, use_global_device_ids=true, to_apply=%region_1.0 | all-reduce | flops 12288 | bytes 98304 | tf_op jit(solution)/shard_map/psum | solution.py:23
  137.6 43.6 %all-gather.4.cloned.1.call-done = bf16[16384,48]{0,1:T(8,128)(2,1)} async-done(((bf16[2048,48]{0,1:T(8,128)(2,1)}), bf16[16384,48]{0,1:T(8,128)(2,1)}) %all-gather.4.cloned.1.call-update) | async-done | bytes 1572880 | tf_op jit(solution)/shard_map/all_gather | solution.py:39
  185.4 10.3 %all-reduce = (f32[128,48]{0,1:T(8,128)S(1)}, f32[48]{0:T(128)S(1)}) all-reduce(f32[128,48]{0,1:T(8,128)S(1)} %convolution_bitcast_fusion.11, f32[48]{0:T(128)S(1)} %get-tuple-element.3), channel_id=1, replica_groups=mesh['row'=8,'feat'=4] {'feat'}, use_global_device_ids=true, to_apply=%region_5.0 | all-reduce | flops 6192 | bytes 49536 | tf_op jit(solution)/shard_map/psum | solution.py:36
  195.7 4.6 convolution_bitcast_fusion.2
  200.9 40.8 %psum.109 = f32[48]{0:T(128)S(1)} all-reduce(f32[48]{0:T(128)S(1)} %multiply_add_fusion.5), channel_id=1, replica_groups=mesh['row'=8,'feat'=4] {'row','feat'}, use_global_device_ids=true, to_apply=%region_8.0 | all-reduce | flops 48 | bytes 384 | tf_op jit(solution)/shard_map/psum | solution.py:50
  241.7 21.1 %psum.107 = f32[48]{0:T(128)S(1)} all-reduce(f32[48]{0:T(128)S(1)} %get-tuple-element.5), channel_id=1, replica_groups=mesh['row'=8,'feat'=4] {'row'}, use_global_device_ids=true, to_apply=%region_4.0 | all-reduce | flops 48 | bytes 384 | tf_op jit(solution)/shard_map/psum | solution.py:27
  262.8 12.3 %reduce-scatter.7.cloned.1.call-done = f32[2048,48]{0,1:T(8,128)} async-done(((f32[16384,48]{0,1:T(8,128)}), f32[2048,48]{0,1:T(8,128)}) %reduce-scatter.7.cloned.1.call-update) | async-done | bytes 393232 | tf_op jit(solution)/shard_map/reduce_scatter | solution.py:12
  279.7 40.7 %psum.110 = f32[256,48]{1,0:T(8,128)S(1)} all-reduce(f32[256,48]{1,0:T(8,128)S(1)} %convolution_bitcast_fusion.7), channel_id=1, replica_groups=mesh['row'=8,'feat'=4] {'row','feat'}, use_global_device_ids=true, to_apply=%region_10.0 | all-reduce | flops 12288 | bytes 98304 | tf_op jit(solution)/shard_map/psum | solution.py:23
  323.2 5.8 psum.111
  329.0 20.4 %psum.112 = f32[48]{0:T(128)S(1)} all-reduce(f32[48]{0:T(128)S(1)} %psum.111), channel_id=1, replica_groups=mesh['row'=8,'feat'=4] {'row'}, use_global_device_ids=true, to_apply=%region_13.0 | all-reduce | flops 48 | bytes 384 | tf_op jit(solution)/shard_map/psum | solution.py:27
  351.4 40.8 %all-gather.6.cloned.1.call-done = bf16[16384,48]{0,1:T(8,128)(2,1)} async-done(((bf16[2048,48]{0,1:T(8,128)(2,1)}), bf16[16384,48]{0,1:T(8,128)(2,1)}) %all-gather.6.cloned.1.call-update) | async-done | bytes 1572880 | tf_op jit(solution)/shard_map/all_gather | solution.py:39
  396.4 10.3 %psum.113 = f32[128,48]{0,1:T(8,128)S(1)} all-reduce(f32[128,48]{0,1:T(8,128)S(1)} %convolution_bitcast_fusion.10), channel_id=1, replica_groups=mesh['row'=8,'feat'=4] {'feat'}, use_global_device_ids=true, to_apply=%region_14.0 | all-reduce | flops 6144 | bytes 49152 | tf_op jit(solution)/shard_map/psum | solution.py:36
  411.4 41.3 %psum.114 = f32[48]{0:T(128)S(1)} all-reduce(f32[48]{0:T(128)S(1)} %multiply_add_fusion.4), channel_id=1, replica_groups=mesh['row'=8,'feat'=4] {'row','feat'}, use_global_device_ids=true, to_apply=%region_17.0 | all-reduce | flops 48 | bytes 384 | tf_op jit(solution)/shard_map/psum | solution.py:50
  452.7 33.1 %reduce-scatter.9.cloned.1.call-done = f32[2048,48]{0,1:T(8,128)} async-done(((f32[16384,48]{0,1:T(8,128)}), f32[2048,48]{0,1:T(8,128)}) %reduce-scatter.9.cloned.1.call-update) | async-done | bytes 393232 | tf_op jit(solution)/shard_map/reduce_scatter | solution.py:12
  490.3 40.8 %psum.115 = f32[256,48]{1,0:T(8,128)S(1)} all-reduce(f32[256,48]{1,0:T(8,128)S(1)} %convolution_bitcast_fusion.6), channel_id=1, replica_groups=mesh['row'=8,'feat'=4] {'row','feat'}, use_global_device_ids=true, to_apply=%region_19.0 | all-reduce | flops 12288 | bytes 98304 | tf_op jit(solution)/shard_map/psum | solution.py:23
  533.1 5.8 psum.116
  538.9 20.4 %psum.117 = f32[48]{0:T(128)S(1)} all-reduce(f32[48]{0:T(128)S(1)} %psum.116), channel_id=1, replica_groups=mesh['row'=8,'feat'=4] {'row'}, use_global_device_ids=true, to_apply=%region_22.0 | all-reduce | flops 48 | bytes 384 | tf_op jit(solution)/shard_map/psum | solution.py:27
  560.3 40.7 %all-gather.8.cloned.1.call-done = bf16[16384,48]{0,1:T(8,128)(2,1)} async-done(((bf16[2048,48]{0,1:T(8,128)(2,1)}), bf16[16384,48]{0,1:T(8,128)(2,1)}) %all-gather.8.cloned.1.call-update) | async-done | bytes 1572880 | tf_op jit(solution)/shard_map/all_gather | solution.py:39
  605.3 10.3 %psum.118 = f32[128,48]{0,1:T(8,128)S(1)} all-reduce(f32[128,48]{0,1:T(8,128)S(1)} %convolution_bitcast_fusion.9), channel_id=1, replica_groups=mesh['row'=8,'feat'=4] {'feat'}, use_global_device_ids=true, to_apply=%region_23.0 | all-reduce | flops 6144 | bytes 49152 | tf_op jit(solution)/shard_map/psum | solution.py:36
  615.5 4.5 convolution_bitcast_fusion
  621.4 41.6 %psum.119 = f32[48]{0:T(128)S(1)} all-reduce(f32[48]{0:T(128)S(1)} %multiply_add_fusion.3), channel_id=1, replica_groups=mesh['row'=8,'feat'=4] {'row','feat'}, use_global_device_ids=true, to_apply=%region_26.0 | all-reduce | flops 48 | bytes 384 | tf_op jit(solution)/shard_map/psum | solution.py:50
  663.0 31.9 %reduce-scatter.11.cloned.1.call-done = f32[2048,48]{0,1:T(8,128)} async-done(((f32[16384,48]{0,1:T(8,128)}), f32[2048,48]{0,1:T(8,128)}) %reduce-scatter.11.cloned.1.call-update) | async-done | bytes 393232 | tf_op jit(solution)/shard_map/reduce_scatter | solution.py:12
  (54 shorter events, 45.8 us)
Async XLA Ops:
  7.2 82.4 %copy-start = (f32[2048,256]{1,0:T(8,128)S(1)}, f32[2048,256]{1,0:T(8,128)}, u32[]{:S(2)}) copy-start(f32[2048,256]{1,0:T(8,128)} %param.7) | copy-start | bytes 6291460
  7.2 82.4 %reduce-scatter.5.cloned.1.call-start = ((), (), s32[]{:S(2)}) async-start(), calls=%async_computation.4 | async-start | bytes 3538944 | tf_op jit(solution)/shard_map/reduce_scatter | solution.py:12
  12.0 122.8 %copy-start.5 = (f32[256]{0:T(256)S(1)}, f32[256]{0:T(256)}, u32[]{:S(2)}) copy-start(f32[256]{0:T(256)} %param.8) | copy-start | bytes 3076
  12.0 169.2 %all-gather.4.cloned.1.call-start = ((), (), s32[]{:S(2)}) async-start(), calls=%async_computation.5 | async-start | bytes 1769472 | tf_op jit(solution)/shard_map/all_gather | solution.py:39
  89.6 45.2 %copy-start.3 = (f32[2048,48]{0,1:T(8,128)S(1)}, f32[2048,48]{0,1:T(8,128)}, u32[]{:S(2)}) copy-start(f32[2048,48]{0,1:T(8,128)} %reduce-scatter.5.cloned.1.call-done) | copy-start | bytes 1179652
  137.5 211.8 %copy-start.1 = (f32[2048,48]{0,1:T(8,128)}, f32[2048,48]{0,1:T(8,128)S(1)}, u32[]{:S(2)}) copy-start(f32[2048,48]{0,1:T(8,128)S(1)} %get-tuple-element.13) | copy-start | bytes 1179652
  137.6 137.6 %reduce-scatter.7.cloned.1.call-start = ((), (), s32[]{:S(2)}) async-start(), calls=%async_computation.6 | async-start | bytes 3538944 | tf_op jit(solution)/shard_map/reduce_scatter | solution.py:12
  200.3 0.7 copy-start.4
  200.3 191.9 %all-gather.6.cloned.1.call-start = ((), (), s32[]{:S(2)}) async-start(), calls=%async_computation.7 | async-start | bytes 1769472 | tf_op jit(solution)/shard_map/all_gather | solution.py:39
  351.3 134.5 %reduce-scatter.9.cloned.1.call-start = ((), (), s32[]{:S(2)}) async-start(), calls=%async_computation.8 | async-start | bytes 3538944 | tf_op jit(solution)/shard_map/reduce_scatter | solution.py:12
  411.2 189.8 %all-gather.8.cloned.1.call-start = ((), (), s32[]{:S(2)}) async-start(), calls=%async_computation.9 | async-start | bytes 1769472 | tf_op jit(solution)/shard_map/all_gather | solution.py:39
  560.3 134.6 %reduce-scatter.11.cloned.1.call-start = ((), (), s32[]{:S(2)}) async-start(), calls=%async_computation.10 | async-start | bytes 3538944 | tf_op jit(solution)/shard_map/reduce_scatter | solution.py:12
  620.1 74.8 %copy-start.2 = (f32[2048,48]{0,1:T(8,128)S(1)}, f32[2048,48]{0,1:T(8,128)}, u32[]{:S(2)}) copy-start(f32[2048,48]{0,1:T(8,128)} %copy-done.1) | copy-start | bytes 1179652
Sparse Core Ops, SparseCore 0:
  12.1 77.4 reduce-scatter.4
  137.7 43.4 all-gather.3
  200.4 74.6 reduce-scatter.6
  351.4 40.6 all-gather.5
  411.3 74.3 reduce-scatter.8
  560.4 40.6 all-gather.7
  620.2 74.5 reduce-scatter.10
